TPU v7x, 256 devices: a whole 4x4x8 slice. The times are simulated.
256 devices in a mesh: gx: 32 (over y_lo, z, core), gy: 8 (over x, y_hi).
Axes of the slice: x: 4, y: 4 (y_hi: 2, y_lo: 2; y = y_hi * 2 + y_lo), z: 8, core: 2. Of those that a mesh axis runs over, the one named last changes fastest.
Arguments:
- velocity: float32 [3, 256, 256, 128], P(None, 'gx', 'gy'), may hold values from -6 to 6
- lm_old: float32 [256, 256, 128], P('gx', 'gy'), may hold values from 0.1 to 10
- mm_old: float32 [256, 256, 128], P('gx', 'gy'), may hold values from 2 to 50
- upstream: int32 [2, 256, 256, 128], P(None, 'gx', 'gy'), may hold values from -3 to 3
- point_pos: float32 [32, 8, 3, 576], P('gx', 'gy'), may hold values from 0 to 128, as said below
- point_coef: float32 [32, 8, 576], P('gx', 'gy'), may hold values from 0.005 to 0.05
- tile_turbines: int32 [32, 8], P('gx', 'gy'), may hold values from 1 to 3, as said below
Outputs:
- lm_next: float32 [256, 256, 128], P('gx', 'gy')
- mm_next: float32 [256, 256, 128], P('gx', 'gy')
- eddy_visc: float32 [256, 256, 128], P('gx', 'gy')
- body_force: float32 [3, 256, 256, 128], P(None, 'gx', 'gy')
Inputs may be any that keep to these rules, and one draw needn't show every extreme that they name: `point_pos`: turbine t of a tile owns slots t * 3 * 64 to (t + 1) * 3 * 64 - 1; its points lie on three blades of radius 12 in a plane of constant x. Every point lies inside its own tile: 0 <= x < 8, 0 < y < 32, and z is within 14 of 64. `tile_turbines`: slots beyond 3 * 64 times a tile's count are unused. Every tile holds at least one turbine; some tile holds 3.
All inputs are finite; a program needn't handle non-finite values.
Results may differ from a plain program's by a relative error of at most 0.0003.
Values sent between devices are 32-bit elements; how exact they have to be, the bound alone decides.
No kernel may reach another device: no remote copies, remote signals or barrier semaphores. Data moves between devices by JAX's collectives and lax.ppermute only.
A program may use at most 128 MiB of HBM per device.

v0:
```python
import math

import jax
import jax.numpy as jnp
from jax import lax
from jax.experimental import pallas as pl
from jax.experimental.pallas import tpu as pltpu
from jax.sharding import PartitionSpec as P

F32 = jnp.float32
CX, CY, NZ = 8, 32, 128
TURBINES, SLOTS = 3, 192
ZLOW, ZSPAN = 46, 40
XMSG = 496
YMSG = 272
YA, YU, YN, YP = 72, 156, 210, 224
EY = 40
PY = 48


def shifted(block, axis, distance):
    count = lax.axis_size(axis)
    return lax.ppermute(block, axis, [(i, (i + distance) % count) for i in range(count)])


def weight(offset):
    scaled = offset * (1.0 / 1.5)
    return jnp.maximum(jnp.exp(-(scaled * scaled)) - math.exp(-4.0), 0.0)


def packed(parts):
    lane = lax.broadcasted_iota(jnp.int32, parts[0].shape, 1)
    first = pltpu.roll(parts[0], NZ - ZLOW, 1)
    second = pltpu.roll(parts[1], NZ + ZSPAN - ZLOW, 1)
    third = pltpu.roll(parts[2], 2 * ZSPAN - ZLOW, 1)
    rest = jnp.where(lane < 3 * ZSPAN, third, 0.0)
    return jnp.where(lane < ZSPAN, first, jnp.where(lane < 2 * ZSPAN, second, rest))


def pack_x(
    vel_in, lm_in, mm_in, pos_in, coef_in, count_in,
    low, high, slab, points, vel, lm, mm, pos, coef, count, sems,
):
    pairs = (
        (vel_in, vel), (pos_in, pos), (coef_in, coef), (count_in, count), (lm_in, lm), (mm_in, mm),
    )
    copies = [pltpu.make_async_copy(x, y, sems.at[i]) for i, (x, y) in enumerate(pairs)]
    for copy in copies:
        copy.start()
    for copy in copies[1:4]:
        copy.wait()
    lane = lax.broadcasted_iota(jnp.int32, (1, 128), 1)
    turbine_count = jnp.broadcast_to(count[...], (1, 128))
    early = lane < 64
    for t in range(TURBINES):
        at = t * SLOTS
        (pos_x, _), (y_first, y_rest), (z_first, z_rest), (s_first, s_rest) = [
            (values[:, at : at + 128], values[:, at + 64 : at + 192])
            for values in (pos[0], pos[1], pos[2], coef[...])
        ]
        live = turbine_count > t
        lines = [
            y_first,
            z_first,
            jnp.where(live, s_first, 0.0),
            jnp.where(early, pltpu.roll(z_rest, 64, 1), y_rest),
            jnp.where(early, pos_x, jnp.where(live, s_rest, 0.0)),
        ]
        block = jnp.concatenate(lines, axis=0)
        for out, base in ((low, 480), (high, 480), (points, 0)):
            out[pl.ds(base + 5 * t, 5), :] = block
    for out, base in ((low, 495), (high, 495), (points, 15)):
        out[pl.ds(base, 1), :] = jnp.zeros((1, 128), F32)
    copies[0].wait()
    for row in range(CX):
        parts = [vel[pl.ds((c * CX + row) * CY, CY), :] for c in range(3)]
        value = packed(parts)
        slab[pl.ds(row * CY, CY), :] = value
        if 2 <= row < 5:
            low[pl.ds(384 + (row - 2) * CY, CY), :] = value
        if 3 <= row < 6:
            high[pl.ds(384 + (row - 3) * CY, CY), :] = value
        for out, first in ((low, 0), (high, CX - 2)):
            if first <= row < first + 2:
                for c in range(3):
                    out[pl.ds(c * 64 + (row - first) * CY, CY), :] = parts[c]
    copies[4].wait()
    copies[5].wait()
    for out, first in ((low, 0), (high, CX - 3)):
        for f, own in enumerate((lm, mm)):
            out[pl.ds(192 + f * 96, 96), :] = own[pl.ds(first * CY, 96), :]


def pack_y(vel, lm, mm, slab, points, xlow, xhigh, low, high, ulow, uhigh):
    for out, message in ((ulow, xlow), (uhigh, xhigh)):
        for i in range(2):
            parts = [message[pl.ds(c * 64 + i * CY, CY), :] for c in range(3)]
            out[pl.ds(i * CY, CY), :] = packed(parts)
    for out, col_v, col_a, col_u in ((low, 0, 0, 0), (high, CY - 2, CY - 3, CY - 5)):
        for c in range(3):
            for j in range(2):
                base, col = (c * 2 + j) * 12, col_v + j
                out[pl.ds(base, 2), :] = xlow[pl.ds(c * 64 + col, 2, stride=CY), :]
                out[pl.ds(base + 2, 8), :] = vel[pl.ds(c * 256 + col, 8, stride=CY), :]
                out[pl.ds(base + 10, 2), :] = xhigh[pl.ds(c * 64 + col, 2, stride=CY), :]
        for f, own in enumerate((lm, mm)):
            for j in range(3):
                base, col = YA + (f * 3 + j) * 14, col_a + j
                out[pl.ds(base, 3), :] = xlow[pl.ds(192 + f * 96 + col, 3, stride=CY), :]
                out[pl.ds(base + 3, 8), :] = own[pl.ds(col, 8, stride=CY), :]
                out[pl.ds(base + 11, 3), :] = xhigh[pl.ds(192 + f * 96 + col, 3, stride=CY), :]
        far, near = (col_u, col_u + 3) if col_v else (col_u + 2, col_u)
        for j in range(3):
            base, col = YU + j * 18, far + j
            out[pl.ds(base, 3), :] = xlow[pl.ds(384 + col, 3, stride=CY), :]
            out[pl.ds(base + 3, 2), :] = ulow[pl.ds(col, 2, stride=CY), :]
            out[pl.ds(base + 5, 8), :] = slab[pl.ds(col, 8, stride=CY), :]
            out[pl.ds(base + 13, 2), :] = uhigh[pl.ds(col, 2, stride=CY), :]
            out[pl.ds(base + 15, 3), :] = xhigh[pl.ds(384 + col, 3, stride=CY), :]
        for j in range(2):
            base, col = YN + j * 6, near + j
            out[pl.ds(base, 3), :] = xlow[pl.ds(384 + col, 3, stride=CY), :]
            out[pl.ds(base + 3, 3), :] = xhigh[pl.ds(384 + col, 3, stride=CY), :]
        out[pl.ds(YN + 12, 2), :] = jnp.zeros((2, 128), F32)
        for k, source in enumerate((points, xlow, xhigh)):
            first = 0 if k == 0 else 480
            out[pl.ds(YP + 15 * k, 15), :] = source[pl.ds(first, 15), :]
        out[pl.ds(YP + 45, 3), :] = jnp.zeros((3, 128), F32)


def expand(source, base, out, out_base, count):
    early = lax.broadcasted_iota(jnp.int32, (1, 128), 1) < 64
    for t in range(count):
        block = source[pl.ds(base + 5 * t, 5), :]
        turned = pltpu.roll(block[3:5, :], 64, 1)
        lines = [
            block[0:1, :],
            block[3:4, :],
            block[1:2, :],
            turned[0:1, :],
            block[2:3, :],
            jnp.where(early, 0.0, block[4:5, :]),
            jnp.where(early, block[4:5, :], turned[1:2, :]),
            jnp.where(early, block[4:5, :], turned[1:2, :]),
        ]
        out[pl.ds(out_base + 8 * t, 8), :] = jnp.concatenate(lines, axis=0)


class Frame:
    def __init__(self, planes, width, turned):
        self.planes, self.width, self.turned = planes, width, turned

    def velocity(self, c, plane, cell):
        return (c * (self.planes + 4) + plane + 2) * self.width + cell + 4

    def average(self, f, plane, cell):
        return (f * (self.planes + 6) + plane + 3) * self.width + cell + 4

    def summed(self, q, plane, cell):
        return (q * (self.planes + 2) + plane + 1) * self.width + cell + 4

    def magnitude(self, plane, cell):
        return plane * self.width + cell + 4

    def sizes(self):
        n, w = self.planes, self.width
        return 3 * (n + 4) * w, 2 * (n + 6) * w, 15 * (n + 2) * w, 3 * (n + 2) * w, n * w


ROWS = Frame(CX, EY, False)
SIDE = Frame(3, 16, True)


def assemble(vel, lm, mm, slab, xlow, xhigh, ulow, uhigh, ev, ea, eu, ends):
    for c in range(3):
        for row in range(CX):
            ev[pl.ds(ROWS.velocity(c, row, 0), CY), :] = vel[pl.ds((c * CX + row) * CY, CY), :]
        for i in range(2):
            ev[pl.ds(ROWS.velocity(c, i - 2, 0), CY), :] = xlow[pl.ds(c * 64 + i * CY, CY), :]
            ev[pl.ds(ROWS.velocity(c, i + 8, 0), CY), :] = xhigh[pl.ds(c * 64 + i * CY, CY), :]
    for f, own in enumerate((lm, mm)):
        for row in range(CX):
            ea[pl.ds(ROWS.average(f, row, 0), CY), :] = own[pl.ds(row * CY, CY), :]
        for i in range(3):
            source = 192 + f * 96 + i * CY
            ea[pl.ds(ROWS.average(f, i - 3, 0), CY), :] = xlow[pl.ds(source, CY), :]
            ea[pl.ds(ROWS.average(f, i + 8, 0), CY), :] = xhigh[pl.ds(source, CY), :]
    zero = jnp.zeros((8, 128), F32)
    for row in range(18):
        eu[pl.ds(row * PY, 8), :] = zero
        eu[pl.ds(row * PY + 40, 8), :] = zero
    for row in range(CX):
        eu[pl.ds((row + 5) * PY + 8, CY), :] = slab[pl.ds(row * CY, CY), :]
    for i in range(3):
        eu[pl.ds(i * PY + 8, CY), :] = xlow[pl.ds(384 + i * CY, CY), :]
        eu[pl.ds((i + 15) * PY + 8, CY), :] = xhigh[pl.ds(384 + i * CY, CY), :]
    for i in range(2):
        eu[pl.ds((i + 3) * PY + 8, CY), :] = ulow[pl.ds(i * CY, CY), :]
        eu[pl.ds((i + 13) * PY + 8, CY), :] = uhigh[pl.ds(i * CY, CY), :]
    for end, (packed_end, tv, ta) in enumerate(ends):
        first = end * (CY - 3)
        for c in range(3):
            for plane in range(-2, 3) if end else range(5):
                source, target = ROWS.velocity(c, 0, first + plane), SIDE.velocity(c, plane, 0)
                for start, count in ((-2, 8), (6, 4)):
                    tv[pl.ds(target + start, count), :] = ev[
                        pl.ds(source + start * EY, count, stride=EY), :
                    ]
        for f in range(2):
            for plane in range(-3, 3) if end else range(6):
                source, target = ROWS.average(f, 0, first + plane), SIDE.average(f, plane, 0)
                for start, count in ((-3, 8), (3, 8)):
                    ta[pl.ds(target + start, count), :] = ea[
                        pl.ds(source + start * EY, count, stride=EY), :
                    ]
        for row in range(18):
            packed_end[pl.ds(row * 16, 16), :] = eu[pl.ds(row * PY + end * 32, 16), :]


def complete(end, message, eu, tv, ta):
    plane_v, plane_a, first = (3, 3, 8) if end else (-2, -3, 3)
    for c in range(3):
        for j in range(2):
            target = SIDE.velocity(c, plane_v + j, -2)
            tv[pl.ds(target, 12), :] = message[pl.ds((c * 2 + j) * 12, 12), :]
    for f in range(2):
        for j in range(3):
            target = SIDE.average(f, plane_a + j, -3)
            ta[pl.ds(target, 14), :] = message[pl.ds(YA + (f * 3 + j) * 14, 14), :]
    far, near = (first + 2, first) if end else (first, first + 3)
    for j in range(3):
        for start, count in ((0, 8), (8, 8), (16, 2)):
            eu[pl.ds(start * 16 + far + j, count, stride=16), :] = message[
                pl.ds(YU + j * 18 + start, count), :
            ]
    for j in range(2):
        for start, source in ((0, 0), (15, 3)):
            eu[pl.ds(start * 16 + near + j, 3, stride=16), :] = message[
                pl.ds(YN + j * 6 + source, 3), :
            ]
        for start, count in ((0, 8), (8, 4)):
            parts = [message[pl.ds((c * 2 + j) * 12 + start, count), :] for c in range(3)]
            eu[pl.ds((start + 3) * 16 + near + j, count, stride=16), :] = packed(parts)


PAIRS = ((0, 0), (1, 1), (2, 2), (0, 1), (0, 2), (1, 2))


def slope_z(values):
    lane = lax.broadcasted_iota(jnp.int32, values.shape, 1)
    above = jnp.where(lane == NZ - 1, values, pltpu.roll(values, NZ - 1, 1))
    below = jnp.where(lane == 0, values, pltpu.roll(values, 1, 1))
    return above - below


def tensor_of(slopes):
    parts = [slopes[0][0], slopes[1][1], slopes[2][2]]
    parts += [slopes[j][i] + slopes[i][j] for i, j in PAIRS[3:]]
    diag = parts[0] * parts[0] + parts[1] * parts[1] + parts[2] * parts[2]
    off = parts[3] * parts[3] + parts[4] * parts[4] + parts[5] * parts[5]
    return parts, jnp.sqrt(2.0 * diag + off)


def closure_first(frame, ev, xs, mags, starts):
    def at(c, plane, cell):
        return ev[pl.ds(frame.velocity(c, plane, cell), 8), :]

    def put(q, plane, cell, value):
        xs[pl.ds(frame.summed(q, plane, cell), 8), :] = value

    for cell in starts:
        before = [at(c, -2, cell) for c in range(3)]
        here = [at(c, -1, cell) for c in range(3)]
        history = []
        for plane in range(-1, frame.planes + 1):
            after = [at(c, plane + 1, cell) for c in range(3)]
            slopes = [
                [after[c] - before[c] for c in range(3)],
                [at(c, plane, cell + 1) - at(c, plane, cell - 1) for c in range(3)],
            ]
            if frame.turned:
                slopes.reverse()
            slopes.append([slope_z(here[c]) for c in range(3)])
            parts, mag = tensor_of(slopes)
            now = [mag * part for part in parts] + [here[i] * here[j] for i, j in PAIRS]
            if 0 <= plane < frame.planes:
                mags[pl.ds(frame.magnitude(plane, cell), 8), :] = mag
            for c in range(3):
                put(12 + c, plane, cell, before[c] + (here[c] + here[c]) + after[c])
            history.append(now)
            if len(history) == 3:
                for q in range(12):
                    value = history[0][q] + (history[1][q] + history[1][q]) + history[2][q]
                    put(q, plane - 1, cell, value)
                history.pop(0)
            before, here = here, after


def closure_hat(frame, xs, uh, starts):
    for c in range(3):
        for plane in range(-1, frame.planes + 1):
            for cell in starts:
                base = frame.summed(12 + c, plane, cell)
                mid = xs[pl.ds(base, 8), :]
                value = xs[pl.ds(base - 1, 8), :] + (mid + mid) + xs[pl.ds(base + 1, 8), :]
                uh[pl.ds(frame.summed(c, plane, cell), 8), :] = value


def take_rows(values, index):
    return jnp.take_along_axis(values, index, axis=0)


def averages_up(frame, ea, shift_plane, shift_cell, plane, cell):
    sub = lax.broadcasted_iota(jnp.int32, (8, 128), 0)
    index = sub - shift_cell + 3
    early = index < 8
    first = jnp.minimum(index, 7)
    second = jnp.maximum(index - 6, 0)
    result = [None, None]
    for shift in range(-3, 4):
        chosen = shift_plane == shift
        for f in range(2):
            base = frame.average(f, plane - shift, cell)
            value = jnp.where(
                early,
                take_rows(ea[pl.ds(base - 3, 8), :], first),
                take_rows(ea[pl.ds(base + 3, 8), :], second),
            )
            result[f] = value if result[f] is None else jnp.where(chosen, value, result[f])
    return result


def closure_last(frame, ea, up, xs, uh, mags, outs, starts, first=0, skipped=0):
    def summed(q, plane, cell):
        base = frame.summed(q, plane, cell)
        mid = xs[pl.ds(base, 8), :]
        return xs[pl.ds(base - 1, 8), :] + (mid + mid) + xs[pl.ds(base + 1, 8), :]

    def hat(c, plane, cell):
        return uh[pl.ds(frame.summed(c, plane, cell), 8), :]

    for plane in range(frame.planes):
        for cell in starts:
            here = [hat(c, plane, cell) for c in range(3)]
            slopes = [
                [hat(c, plane + 1, cell) - hat(c, plane - 1, cell) for c in range(3)],
                [hat(c, plane, cell + 1) - hat(c, plane, cell - 1) for c in range(3)],
            ]
            shifts = [
                pl.ds(d * CX * CY + plane * CY + cell, 8)
                if not frame.turned
                else pl.ds(d * CX * CY + cell * CY + first + plane, 8, stride=CY)
                for d in range(2)
            ]
            if frame.turned:
                slopes.reverse()
                shifts.reverse()
            slopes.append([slope_z(here[c]) for c in range(3)])
            parts, mag = tensor_of(slopes)
            mag = 0.25 * mag
            lm_sum = diag = off = None
            for q, (i, j) in enumerate(PAIRS):
                model = summed(q, plane, cell) - mag * parts[q]
                leonard = summed(6 + q, plane, cell) - (1.0 / 16.0) * (here[i] * here[j])
                term = leonard * model
                lm_sum = term if lm_sum is None else lm_sum + term
                square = model * model
                if q < 3:
                    diag = square if diag is None else diag + square
                else:
                    off = square if off is None else off + square
            lm_term = lm_sum * (1.0 / 512.0)
            mm_term = (2.0 * diag + off) * (1.0 / 2048.0)
            lm_up, mm_up = averages_up(frame, ea, up[shifts[0], :], up[shifts[1], :], plane, cell)
            ratio = (0.2 / 1.5) * jnp.sqrt(jnp.sqrt(jnp.sqrt(lm_up * mm_up)))
            inverse = 1.0 / (1.0 + ratio)
            lm_new = jnp.maximum((ratio * lm_term + lm_up) * inverse, 0.0)
            mm_new = (ratio * mm_term + mm_up) * inverse
            smag = 0.5 * mags[pl.ds(frame.magnitude(plane, cell), 8), :]
            if frame.turned:
                where_at = pl.ds(skipped + plane, 8, stride=8)
            else:
                where_at = pl.ds(plane * CY + cell, 8)
            for out, value in zip(outs, (lm_new, mm_new, lm_new / mm_new * smag)):
                out[where_at, :] = value


def split(values):
    high = values.astype(jnp.bfloat16)
    return high, (values - high.astype(F32)).astype(jnp.bfloat16)


def dot_over(a, b, dims):
    (a_high, a_low), (b_high, b_low) = split(a), split(b)

    def dot(x, y):
        return lax.dot_general(x, y, (dims, ((), ())), preferred_element_type=F32)

    return dot(a_high, b_high) + dot(a_high, b_low) + dot(a_low, b_high)


def turbines(blocks, shift_x, shift_y, in_rows, first, span, out_rows, out_at, eu, total, keep):
    begin, stride, columns_out = out_at
    cell_x = lax.broadcasted_iota(jnp.int32, (24, 128), 0).astype(F32) - 5.0 - shift_x
    cell_y = lax.broadcasted_iota(jnp.int32, (span, 256), 0).astype(F32) + shift_y
    cell_z = lax.broadcasted_iota(jnp.int32, (ZSPAN, 256), 0).astype(F32) + float(ZLOW)
    weights_x = [weight(cell_x - block[6:7, :]) for block in blocks]
    planes = [None] * len(blocks)
    for row in in_rows:
        values = eu[pl.ds((row + 5) * PY + first, span), :]
        for t, weight_x in enumerate(weights_x):
            term = weight_x[row + 5 : row + 6, :] * values
            planes[t] = term if planes[t] is None else planes[t] + term
    patches = []
    for block, plane in zip(blocks, planes):
        pos_y = jnp.concatenate([block[0:1, :], block[1:2, :]], axis=1)
        pos_z = jnp.concatenate([block[2:3, :], block[3:4, :]], axis=1)
        strength = jnp.concatenate([block[4:5, :], block[5:6, :]], axis=1)
        strength = jnp.where(keep(pos_y), strength, 0.0)
        weight_y = weight(cell_y - pos_y)
        weight_z = weight(cell_z - pos_z)
        columns = dot_over(plane.T, weight_y, ((1,), (0,)))
        sampled = [
            jnp.sum(columns[c * ZSPAN : (c + 1) * ZSPAN, :] * weight_z, axis=0, keepdims=True)
            for c in range(3)
        ]
        speed = jnp.sqrt(sampled[0] * sampled[0] + sampled[1] * sampled[1] + sampled[2] * sampled[2])
        scale = -(strength * speed)
        spread = [weight_z * (scale * sampled[c]) for c in range(3)]
        spread = jnp.concatenate(spread + [jnp.zeros((8, 256), F32)], axis=0)
        rows_y = weight_y[8 : 8 + CY, :] if columns_out == CY else weight_y
        patches.append(dot_over(rows_y, spread, ((1,), (1,))))
    for row in out_rows:
        where_at = pl.ds(row * stride + begin, columns_out)
        value = total[where_at, :]
        for weight_x, patch in zip(weights_x, patches):
            value = value + weight_x[row + 5 : row + 6, :] * patch
        total[where_at, :] = value


def inside(pos_y):
    return (pos_y >= 2.0) & (pos_y <= float(CY - 3))


def unpack(values):
    lane = lax.broadcasted_iota(jnp.int32, values.shape, 1)
    held = (lane >= ZLOW) & (lane < ZLOW + ZSPAN)
    shifts = (ZLOW, NZ + ZLOW - ZSPAN, NZ + ZLOW - 2 * ZSPAN)
    return [jnp.where(held, pltpu.roll(values, shift % NZ, 1), 0.0) for shift in shifts]


def interior(
    vel, lm, mm, up, slab, points, xlow, xhigh, ulow, uhigh,
    results, forces, expanded, *refs,
):
    ends = refs[:5], refs[5:10]
    ev, ea, xs, uh, mags, total, eu = refs[10:]
    assemble(vel, lm, mm, slab, xlow, xhigh, ulow, uhigh, ev, ea, eu, [end[2:] for end in ends])
    closure_first(ROWS, ev, xs, mags, (1, 9, 17, 23))
    closure_hat(ROWS, xs, uh, (2, 10, 18, 22))
    field = CX * CY
    outs = [results.at[pl.ds(i * field, field), :] for i in range(3)]
    closure_last(ROWS, ea, up, xs, uh, mags, outs, (3, 11, 19, 21))
    total[...] = jnp.zeros((field, 128), F32)
    for k, source in enumerate((points, xlow, xhigh)):
        expand(source, 480 if k else 0, expanded, 24 * k, TURBINES)
    for base, shift_x, in_rows, out_rows in (
        (0, 0.0, range(-2, 11), range(0, 8)),
        (24, -8.0, range(-5, 3), range(0, 3)),
        (48, 8.0, range(6, 13), range(6, 8)),
    ):
        blocks = [expanded[pl.ds(base + t * 8, 8), :] for t in range(TURBINES)]
        turbines(blocks, shift_x, -8.0, in_rows, 0, PY, out_rows, (0, CY, CY), eu, total, inside)
    for row in range(CX):
        values = total[pl.ds(row * CY, CY), :]
        for c, out in enumerate(unpack(values)):
            forces[pl.ds((c * CX + row) * CY, CY), :] = out
        for end, (rim, total_rim, *_) in enumerate(ends):
            col = end * (CY - 8)
            total_rim[pl.ds(row * 16 + 8 - 8 * end, 8), :] = values[col : col + 8, :]
            for i in range(3):
                rim[pl.ds((i * CX + row) * 8, 8), :] = results[
                    pl.ds(i * field + row * CY + col, 8), :
                ]


def rim_hits(end, everyone):
    lines = []
    place = lax.broadcasted_iota(jnp.int32, (9, 128), 0)
    left = (place >= 3) & (place < 6)
    least, most = jnp.where(left, 5.0, -1.0), jnp.where(place < 6, float(CX + 1), 2.0)
    for beyond in range(2):

        def line(q, base=72 * beyond):
            parts = everyone[pl.ds(base + q, 8, stride=8), :], everyone[pl.ds(base + 64 + q, 1), :]
            return jnp.concatenate(parts, axis=0)

        hit = None
        for half in range(2):
            pos_y = line(half)
            found = (pos_y > float(CY - 3)) if end != beyond else (pos_y < 2.0)
            found = found & (line(4 + half) > 0.0)
            hit = found if hit is None else hit | found
        pos_x = line(6)
        hit = hit & (pos_x > least) & (pos_x < most)
        lines.append(jnp.max(hit.astype(F32), axis=1, keepdims=True))
    bits = lax.shift_left(
        jnp.ones((9, 1), jnp.int32), lax.broadcasted_iota(jnp.int32, (9, 1), 0)
    ).astype(F32)
    return jnp.sum(bits * (lines[0] + 512.0 * lines[1])).astype(jnp.int32)


def stacked_product(a, b, dims, axes):
    (a_high, a_low), (b_high, b_low) = split(a), split(b)
    a_terms = jnp.concatenate([a_high, a_high, a_low], axis=axes[0])
    b_terms = jnp.concatenate([b_high, b_low, b_high], axis=axes[1])
    return lax.dot_general(a_terms, b_terms, (dims, ((), ())), preferred_element_type=F32)


def rim_batch(end, items, eu, total, everyone):
    cell_x = lax.broadcasted_iota(jnp.int32, (24, 128), 0).astype(F32) - 5.0
    cell_y = lax.broadcasted_iota(jnp.int32, (16, 256), 0).astype(F32)
    cell_z = lax.broadcasted_iota(jnp.int32, (ZSPAN, 256), 0).astype(F32) + float(ZLOW)
    ready = []
    for item in items:
        beyond = item >= 9
        place = jnp.where(beyond, item - 9, item)
        block = everyone[pl.ds(pl.multiple_of(item * 8, 8), 8), :]
        shift_x = jnp.where(place < 3, 0.0, jnp.where(place < 6, -8.0, 8.0))
        late = jnp.logical_not(beyond) if end else beyond
        shift_y = jnp.where(late, 24.0, -8.0)
        lowest = jnp.where(late, float(CY - 3), -1.0)
        highest = jnp.where(late, float(CY + 1), 2.0)
        weight_x = weight(cell_x - shift_x - block[6:7, :])
        terms = [weight_x[row : row + 1, :] * eu[pl.ds(row * 16, 16), :] for row in range(18)]
        while len(terms) > 1:
            terms = [sum(terms[i + 1 : i + 2], terms[i]) for i in range(0, len(terms), 2)]
        pos_y = jnp.concatenate([block[0:1, :], block[1:2, :]], axis=1)
        pos_z = jnp.concatenate([block[2:3, :], block[3:4, :]], axis=1)
        strength = jnp.concatenate([block[4:5, :], block[5:6, :]], axis=1)
        strength = jnp.where((pos_y > lowest) & (pos_y < highest), strength, 0.0)
        weights = weight(cell_y + shift_y - pos_y), weight(cell_z - pos_z)
        ready.append((weight_x, terms[0], *weights, strength))
    patches = []
    for _, plane, weight_y, weight_z, strength in ready:
        columns = stacked_product(plane.T, weight_y, ((1,), (0,)), (1, 0))
        sampled = [
            jnp.sum(columns[c * ZSPAN : (c + 1) * ZSPAN, :] * weight_z, axis=0, keepdims=True)
            for c in range(3)
        ]
        speed = jnp.sqrt(sampled[0] * sampled[0] + sampled[1] * sampled[1] + sampled[2] * sampled[2])
        scale = -(strength * speed)
        spread = [weight_z * (scale * sampled[c]) for c in range(3)]
        spread = jnp.concatenate(spread + [jnp.zeros((8, 256), F32)], axis=0)
        patches.append(stacked_product(weight_y, spread, ((1,), (1,)), (1, 1)))
    for row in range(CX):
        value = total[pl.ds(row * 16, 16), :]
        for patch, (weight_x, *_) in zip(patches, ready):
            value = value + weight_x[row + 5 : row + 6, :] * patch
        total[pl.ds(row * 16, 16), :] = value


def finish(end, inputs, scratch, results, forces, closed, forced):
    up, expanded, message, rim_in, total_in, eu_in, tv_in, ta_in = inputs
    tv, ta, eu, xs, uh, mags, total, everyone, listed = scratch
    everyone[pl.ds(0, 72), :] = expanded[...]
    expand(message, YP, everyone, 72, 3 * TURBINES)
    everyone[pl.ds(144, 8), :] = jnp.zeros((8, 128), F32)
    hits = rim_hits(end, everyone)
    found = jnp.int32(0)
    for item in range(18):
        listed[found] = jnp.int32(item)
        found = found + lax.rem(lax.shift_right_logical(hits, item), 2)
    for i in range(3):
        listed[found + i] = jnp.int32(18)
    tv[...] = tv_in[...]
    ta[...] = ta_in[...]
    eu[...] = eu_in[...]
    total[...] = total_in[...]
    results[...] = rim_in[...]
    complete(end, message, eu, tv, ta)
    closure_first(SIDE, tv, xs, mags, (-2, 2))
    closure_hat(SIDE, xs, uh, (-1, 1))
    outs = [results.at[pl.ds(i * 64, 64), :] for i in range(3)]
    first, skipped = (CY - 3, 5) if end else (0, 0)
    closure_last(SIDE, ta, up, xs, uh, mags, outs, (0,), first, skipped)
    closed()

    def batch(i, carry):
        rim_batch(end, [listed[3 * i + t] for t in range(3)], eu, total, everyone)
        return carry

    def write():
        for row in range(CX):
            values = total[pl.ds(row * 16 + 8 - 8 * end, 8), :]
            for c, out in enumerate(unpack(values)):
                forces[pl.ds((c * CX + row) * 8, 8), :] = out

    if end == 0:
        lax.fori_loop(0, lax.div(found + 2, 3), batch, 0)
        write()
        return

    @pl.when(found > 0)
    def _():
        lax.fori_loop(0, lax.div(found + 2, 3), batch, 0)
        write()
        forced()


def edge_low(*refs):
    inner_results, inner_forces, results, forces = refs[8:12]
    *scratch, sems = refs[16:]
    field = CX * CY
    sources = [inner_results.at[pl.ds(i * field, field), :] for i in range(3)] + [inner_forces]
    copies = [
        pltpu.make_async_copy(source.reshape(*target.shape), target, sems.at[i])
        for i, (source, target) in enumerate(zip(sources, refs[12:16]))
    ]
    for copy in copies:
        copy.start()
    finish(0, refs[:8], scratch, results, forces, lambda: None, None)
    for copy in copies:
        copy.wait()


def edge_high(*refs):
    inputs, (low_results, low_forces), targets = refs[:8], refs[8:10], refs[14:18]
    results, forces, sems = refs[27:]
    copies = []

    def sent(source, target, i, end):
        columns = pl.ds(end * (CY - 8), 8)
        source = source.reshape(*target.shape[:-2], 8, NZ)
        return pltpu.make_async_copy(source, target.at[..., columns, :], sems.at[i])

    def fields(values, end):
        for i, target in enumerate(targets[:3]):
            copies.append(sent(values.at[pl.ds(i * 64, 64), :], target, len(copies), end))
            copies[-1].start()

    def forced():
        copy = sent(forces, targets[3], 7, 1)
        copy.start()
        copy.wait()

    fields(low_results, 0)
    copies.append(sent(low_forces, targets[3], len(copies), 0))
    copies[-1].start()
    finish(1, inputs, refs[18:27], results, forces, lambda: fields(results, 1), forced)
    for copy in copies:
        copy.wait()


VMEM = pl.BlockSpec(memory_space=pltpu.VMEM)
HBM = pl.BlockSpec(memory_space=pltpu.HBM)


def rows(count):
    return jax.ShapeDtypeStruct((count, 128), F32)


def limit(mebibytes):
    return pltpu.CompilerParams(vmem_limit_bytes=mebibytes * 1024 * 1024)


def shards(velocity, lm_old, mm_old, upstream, point_pos, point_coef, tile_turbines):
    field = CX * CY
    up = upstream.reshape(2 * field, NZ)
    inputs = (
        velocity.reshape(3 * field, NZ),
        lm_old.reshape(field, NZ),
        mm_old.reshape(field, NZ),
        point_pos.reshape(3, 1, TURBINES * SLOTS),
        point_coef[0],
    )
    low, high, slab, points, vel, lm, mm = pl.pallas_call(
        pack_x,
        out_shape=[rows(n) for n in (XMSG, XMSG, field, 16, 3 * field, field, field)],
        in_specs=[HBM] * 5 + [pl.BlockSpec(memory_space=pl.ANY)],
        out_specs=[VMEM] * 7,
        scratch_shapes=[
            pltpu.VMEM((3, 1, TURBINES * SLOTS), F32),
            pltpu.VMEM((1, TURBINES * SLOTS), F32),
            pltpu.VMEM((1, 1), jnp.int32),
            pltpu.SemaphoreType.DMA((6,)),
        ],
        compiler_params=limit(8),
        name="pack_x",
    )(*(pltpu.with_memory_space_constraint(value, pltpu.HBM) for value in inputs), tile_turbines)
    xlow = shifted(high, "gx", 1)
    xhigh = shifted(low, "gx", -1)
    low, high, ulow, uhigh = pl.pallas_call(
        pack_y,
        out_shape=(rows(YMSG), rows(YMSG), rows(64), rows(64)),
        in_specs=[VMEM] * 7,
        out_specs=(VMEM,) * 4,
        compiler_params=limit(8),
        name="pack_y",
    )(vel, lm, mm, slab, points, xlow, xhigh)
    ylow = shifted(high, "gy", 1)
    yhigh = shifted(low, "gy", -1)
    size_v, size_a, *sizes = SIDE.sizes()
    handed = [3 * 64, CX * 16, 18 * 16, size_v, size_a]
    work = [*ROWS.sizes(), field, 18 * PY]
    first = pl.pallas_call(
        interior,
        out_shape=[rows(n) for n in (3 * field, 3 * field, 9 * 8, *handed, *handed)],
        in_specs=[VMEM] * 10,
        out_specs=[VMEM] * 13,
        scratch_shapes=[pltpu.VMEM((n, 128), F32) for n in work],
        compiler_params=limit(16),
        cost_estimate=pl.CostEstimate(flops=20_000_000, bytes_accessed=20_000_000, transcendentals=0),
        name="interior",
    )(vel, lm, mm, up, slab, points, xlow, xhigh, ulow, uhigh)
    shape = (CX, CY, NZ)
    shapes = [shape, shape, shape, (3, *shape)]
    _, _, eu, tv, ta = handed
    own = [tv, ta, eu, *sizes, CX * 16, 19 * 8]
    own = [pltpu.VMEM((n, 128), F32) for n in own] + [pltpu.SMEM((24,), jnp.int32)]
    cost = pl.CostEstimate(flops=4_000_000, bytes_accessed=4_000_000, transcendentals=0)
    *low, lm_next, mm_next, visc, body = pl.pallas_call(
        edge_low,
        out_shape=[rows(3 * 64)] * 2 + [pltpu.HBM(s, F32) for s in shapes],
        in_specs=[VMEM] * 10,
        out_specs=[VMEM] * 2 + [HBM] * 4,
        scratch_shapes=own + [pltpu.SemaphoreType.DMA((4,))],
        compiler_params=limit(16),
        cost_estimate=cost,
        name="edge_low",
    )(up, first[2], ylow, *first[3:8], *first[:2])
    given = [
        pltpu.with_memory_space_constraint(value, pltpu.HBM)
        for value in (lm_next, mm_next, visc, body)
    ]
    return pl.pallas_call(
        edge_high,
        out_shape=[pltpu.HBM(s, F32) for s in shapes],
        in_specs=[VMEM] * 10 + [HBM] * 4,
        out_specs=[HBM] * 4,
        input_output_aliases={10 + i: i for i in range(4)},
        scratch_shapes=own
        + [pltpu.VMEM((3 * 64, 128), F32)] * 2
        + [pltpu.SemaphoreType.DMA((8,))],
        compiler_params=limit(16),
        cost_estimate=cost,
        name="edge_high",
    )(up, first[2], yhigh, *first[8:13], *low, *given)


def solution(mesh):
    return jax.shard_map(
        shards,
        mesh=mesh,
        in_specs=(
            P(None, "gx", "gy", None),
            P("gx", "gy", None),
            P("gx", "gy", None),
            P(None, "gx", "gy", None),
            P("gx", "gy", None, None),
            P("gx", "gy", None),
            P("gx", "gy"),
        ),
        out_specs=(
            P("gx", "gy", None),
            P("gx", "gy", None),
            P("gx", "gy", None),
            P(None, "gx", "gy", None),
        ),
        check_vma=False,
    )
```

profile of v0, /device:TPU:24, one launch (start us, length us, event | category | flops | bytes accessed | tf_op | source)
XLA Modules:
  0.0 25.2 jit_solution(9652210287893461202)
XLA Ops:
  1.3 1.2 %pack_x.1 = (f32[496,128]{1,0:T(8,128)S(1)}, f32[496,128]{1,0:T(8,128)S(1)}, f32[256,128]{1,0:T(8,128)S(1)}, f32[16,128]{1,0:T(8,128)S(1)}, f32[768,128]{1,0:T(8...) custom-call(f32[768,128]{1,0:T(8,128)} %bitcast.9, f32[256,128]{1,0:T(8,128)} %bitcast.10, ...), custom_call_target="tpu_custom_call" | custom-call | tf_op jit(solution)/shard_map/pack_x/pallas_call | solution.py:677
  2.5 0.1 collective-permute-start
  2.6 5.6 %collective-permute-start.1 = (f32[496,128]{1,0:T(8,128)S(1)}, f32[496,128]{1,0:T(8,128)S(1)}, u32[]{:S(2)}, u32[]{:S(2)}) collective-permute-start(f32[496,128]{1,0:T(8,128)S(1)} %get-tuple-element.40), channel_id=1, source_target_pairs={{0,248},{8,0},{16,8},{24,16},{32,24},{40,32},{48,40},{56,48},{64,5... | collective-permute-start | bytes 761864 | tf_op jit(solution)/shard_map/ppermute | solution.py:23
  8.2 3.9 %collective-permute-done.xlow = f32[496,128]{1,0:T(8,128)S(1)} collective-permute-done((f32[496,128]{1,0:T(8,128)S(1)}, f32[496,128]{1,0:T(8,128)S(1)}, u32[]{:S(2)}, u32[]{:S(2)}) %collective-permute-start) | collective-permute-done | bytes 253984 | tf_op jit(solution)/shard_map/ppermute | solution.py:23
  12.0 0.0 collective-permute-done.1.xhigh
  12.0 0.0 copy-start
  12.1 0.2 pack_y.1
  12.2 1.9 %collective-permute-start.3 = (f32[272,128]{1,0:T(8,128)S(1)}, f32[272,128]{1,0:T(8,128)S(1)}, u32[]{:S(2)}, u32[]{:S(2)}) collective-permute-start(f32[272,128]{1,0:T(8,128)S(1)} %get-tuple-element.50), channel_id=1, source_target_pairs={{0,1},{1,2},{2,3},{3,4},{4,5},{5,6},{6,7},{7,0},{8,9},{9,10},{10,1... | collective-permute-start | bytes 417800 | tf_op jit(solution)/shard_map/ppermute | solution.py:23
  14.2 1.7 %collective-permute-start.2 = (f32[272,128]{1,0:T(8,128)S(1)}, f32[272,128]{1,0:T(8,128)S(1)}, u32[]{:S(2)}, u32[]{:S(2)}) collective-permute-start(f32[272,128]{1,0:T(8,128)S(1)} %get-tuple-element.44), channel_id=1, source_target_pairs={{0,7},{1,0},{2,1},{3,2},{4,3},{5,4},{6,5},{7,6},{8,15},{9,8},{10,9... | collective-permute-start | bytes 417800 | tf_op jit(solution)/shard_map/ppermute | solution.py:23
  15.8 0.0 copy-done
  15.8 3.4 %interior.1 = (f32[768,128]{1,0:T(8,128)S(1)}, f32[768,128]{1,0:T(8,128)S(1)}, f32[72,128]{1,0:T(8,128)S(1)}, f32[192,128]{1,0:T(8,128)S(1)}, f32[128,128]{1,0:T...) custom-call(f32[768,128]{1,0:T(8,128)S(1)} %get-tuple-element.34.vel, ...), custom_call_target="tpu_custom_call" | custom-call | flops 20000000 | bytes 20000000 | tf_op jit(solution)/shard_map/interior/pallas_call | solution.py:706
  19.2 2.6 %collective-permute-done.3.refs_2_ = f32[272,128]{1,0:T(8,128)S(1)} collective-permute-done((f32[272,128]{1,0:T(8,128)S(1)}, f32[272,128]{1,0:T(8,128)S(1)}, u32[]{:S(2)}, u32[]{:S(2)}) %collective-permute-start.3) | collective-permute-done | bytes 139296 | tf_op jit(solution)/shard_map/ppermute | solution.py:23
  21.8 1.3 %edge_low.1 = (f32[192,128]{1,0:T(8,128)S(1)}, f32[192,128]{1,0:T(8,128)S(1)}, f32[8,32,128]{2,1,0:T(8,128)}, f32[8,32,128]{2,1,0:T(8,128)}, f32[8,32,128]{2,1,0:T(8,128)}, /*index=5*/f32[3,8,32,128]{3,2,1,0:T(8,128)}) custom-call(s32[512,128]{1,0:T(8,128)S(1)} %bitcast.7, f32[72,128]{1,0:T(8,128)S(1)} %get-tuple-element.43.refs_1_, ...), custom_call_target="tpu_custom_call" | custom-call | flops 4000000 | bytes 4000000 | tf_op jit(solution)/shard_map/edge_low/pallas_call | solution.py:722
  23.2 0.0 collective-permute-done.2.refs_2_
  23.2 2.1 %edge_high.1 = (f32[8,32,128]{2,1,0:T(8,128)}, f32[8,32,128]{2,1,0:T(8,128)}, f32[8,32,128]{2,1,0:T(8,128)}, f32[3,8,32,128]{3,2,1,0:T(8,128)}) custom-call(s32[512,128]{1,0:T(8,128)S(1)} %bitcast.8, f32[72,128]{1,0:T(8,128)S(1)} %get-tuple-element.43.refs_1_, ...), custom_call_target="tpu_custom_call", output_to_operand_aliasing={{0}: (10, {}), {1}: (11, {}), {2}: (12, {}), {3}: (13, {})} | custom-call | flops 4000000 | bytes 4000000 | tf_op jit(solution)/shard_map/edge_high/pallas_call | solution.py:736
Async XLA Ops:
  2.5 9.5 %collective-permute-start = (f32[496,128]{1,0:T(8,128)S(1)}, f32[496,128]{1,0:T(8,128)S(1)}, u32[]{:S(2)}, u32[]{:S(2)}) collective-permute-start(f32[496,128]{1,0:T(8,128)S(1)} %get-tuple-element.39), channel_id=1, source_target_pairs={{0,8},{8,16},{16,24},{24,32},{32,40},{40,48},{48,56},{56,64},{64,7... | collective-permute-start | bytes 761864 | tf_op jit(solution)/shard_map/ppermute | solution.py:23
  2.6 9.4 %collective-permute-start.1 = (f32[496,128]{1,0:T(8,128)S(1)}, f32[496,128]{1,0:T(8,128)S(1)}, u32[]{:S(2)}, u32[]{:S(2)}) collective-permute-start(f32[496,128]{1,0:T(8,128)S(1)} %get-tuple-element.40), channel_id=1, source_target_pairs={{0,248},{8,0},{16,8},{24,16},{32,24},{40,32},{48,40},{56,48},{64,5... | collective-permute-start | bytes 761864 | tf_op jit(solution)/shard_map/ppermute | solution.py:23
  12.0 3.8 %copy-start = (s32[2,8,32,128]{3,2,1,0:T(8,128)S(1)}, s32[2,8,32,128]{3,2,1,0:T(8,128)}, u32[]{:S(2)}) copy-start(s32[2,8,32,128]{3,2,1,0:T(8,128)} %param.10) | copy-start | bytes 786436
  12.2 9.6 %collective-permute-start.3 = (f32[272,128]{1,0:T(8,128)S(1)}, f32[272,128]{1,0:T(8,128)S(1)}, u32[]{:S(2)}, u32[]{:S(2)}) collective-permute-start(f32[272,128]{1,0:T(8,128)S(1)} %get-tuple-element.50), channel_id=1, source_target_pairs={{0,1},{1,2},{2,3},{3,4},{4,5},{5,6},{6,7},{7,0},{8,9},{9,10},{10,1... | collective-permute-start | bytes 417800 | tf_op jit(solution)/shard_map/ppermute | solution.py:23
  14.2 9.0 %collective-permute-start.2 = (f32[272,128]{1,0:T(8,128)S(1)}, f32[272,128]{1,0:T(8,128)S(1)}, u32[]{:S(2)}, u32[]{:S(2)}) collective-permute-start(f32[272,128]{1,0:T(8,128)S(1)} %get-tuple-element.44), channel_id=1, source_target_pairs={{0,7},{1,0},{2,1},{3,2},{4,3},{5,4},{6,5},{7,6},{8,15},{9,8},{10,9... | collective-permute-start | bytes 417800 | tf_op jit(solution)/shard_map/ppermute | solution.py:23
where the time goes:
time: 25.3 us; the launch traced here: 25.2 us
  starting transfers between devices  9.24 us (37%)
  Pallas kernels  8.14 us (32%)
  waiting for transfers between devices  6.53 us (26%)
  between operations  1.32 us (5%)
    ppermute x4, starting transfers between devices, shifted(): lax.ppermute(block, axis, [(i, (i + distance) % count) for i in range(cou...  9.24 us
    ppermute x4, waiting for transfers between devices, shifted(): lax.ppermute(block, axis, [(i, (i + distance) % count) for i in range(cou...  6.53 us
    pallas_call x1, Pallas kernels, shards(): pl.pallas_call(interior, out_shape=[rows(n) for n in (3 * field, 3 * fiel...  3.36 us
    pallas_call x1, Pallas kernels, shards(): pl.pallas_call(edge_high, out_shape=[pltpu.HBM(s, F32) for s in shapes],...  2.07 us
    pallas_call x1, Pallas kernels, shards(): pl.pallas_call(edge_low, out_shape=[rows(3 * 64)] * 2 + [pltpu.HBM(s, F32...  1.31 us
    pallas_call x1, Pallas kernels, shards(): pl.pallas_call(pack_x, out_shape=[rows(n) for n in (XMSG, XMSG, field, 16...  1.24 us
  transfers between devices with their start and end apart: 4, of which 2 were waited for; matrix products, arithmetic and copies ran while one was open for 0% of the time, Pallas kernels for 19%

commit v1 on v0

--- a/solution.py
+++ b/solution.py
@@ -560,7 +560,7 @@
         total[pl.ds(row * 16, 16), :] = value
 
 
-def finish(end, inputs, scratch, results, forces, closed, forced):
+def finish(end, inputs, scratch, results, forces, closed):
     up, expanded, message, rim_in, total_in, eu_in, tv_in, ta_in = inputs
     tv, ta, eu, xs, uh, mags, total, everyone, listed = scratch
     everyone[pl.ds(0, 72), :] = expanded[...]
@@ -590,64 +590,49 @@
         rim_batch(end, [listed[3 * i + t] for t in range(3)], eu, total, everyone)
         return carry
 
-    def write():
-        for row in range(CX):
-            values = total[pl.ds(row * 16 + 8 - 8 * end, 8), :]
-            for c, out in enumerate(unpack(values)):
-                forces[pl.ds((c * CX + row) * 8, 8), :] = out
-
-    if end == 0:
-        lax.fori_loop(0, lax.div(found + 2, 3), batch, 0)
-        write()
-        return
-
-    @pl.when(found > 0)
+    @pl.when(found == 1)
+    def _():
+        rim_batch(end, [listed[0]], eu, total, everyone)
+
+    @pl.when(found > 1)
     def _():
         lax.fori_loop(0, lax.div(found + 2, 3), batch, 0)
-        write()
-        forced()
+
+    for row in range(CX):
+        values = total[pl.ds(row * 16 + 8 - 8 * end, 8), :]
+        for c, out in enumerate(unpack(values)):
+            forces[pl.ds((c * CX + row) * 8, 8), :] = out
 
 
 def edge_low(*refs):
-    inner_results, inner_forces, results, forces = refs[8:12]
-    *scratch, sems = refs[16:]
-    field = CX * CY
-    sources = [inner_results.at[pl.ds(i * field, field), :] for i in range(3)] + [inner_forces]
-    copies = [
-        pltpu.make_async_copy(source.reshape(*target.shape), target, sems.at[i])
-        for i, (source, target) in enumerate(zip(sources, refs[12:16]))
-    ]
-    for copy in copies:
-        copy.start()
-    finish(0, refs[:8], scratch, results, forces, lambda: None, None)
-    for copy in copies:
-        copy.wait()
+    finish(0, refs[:8], refs[10:], refs[8], refs[9], lambda: None)
 
 
 def edge_high(*refs):
-    inputs, (low_results, low_forces), targets = refs[:8], refs[8:10], refs[14:18]
-    results, forces, sems = refs[27:]
+    low_results, low_forces, inner_results, inner_forces = refs[8:12]
+    targets, scratch = refs[12:16], refs[16:25]
+    results, forces, sems = refs[25:]
     copies = []
 
-    def sent(source, target, i, end):
-        columns = pl.ds(end * (CY - 8), 8)
-        source = source.reshape(*target.shape[:-2], 8, NZ)
-        return pltpu.make_async_copy(source, target.at[..., columns, :], sems.at[i])
-
-    def fields(values, end):
+    def send(source, target, first, count):
+        target = target.at[..., pl.ds(first, count), :]
+        copies.append(pltpu.make_async_copy(source, target, sems.at[len(copies)]))
+        copies[-1].start()
+
+    def fields(values, first):
         for i, target in enumerate(targets[:3]):
-            copies.append(sent(values.at[pl.ds(i * 64, 64), :], target, len(copies), end))
-            copies[-1].start()
-
-    def forced():
-        copy = sent(forces, targets[3], 7, 1)
-        copy.start()
-        copy.wait()
-
+            send(values.at[pl.ds(i * 64, 64), :].reshape(CX, 8, NZ), target, first, 8)
+
+    middle = pl.ds(8, CY - 16)
+    send(inner_forces.reshape(3, CX, CY, NZ).at[:, :, middle, :], targets[3], 8, CY - 16)
+    part = CX * CY
+    for i, target in enumerate(targets[:3]):
+        source = inner_results.at[pl.ds(i * part, part), :].reshape(CX, CY, NZ)
+        send(source.at[:, middle, :], target, 8, CY - 16)
     fields(low_results, 0)
-    copies.append(sent(low_forces, targets[3], len(copies), 0))
-    copies[-1].start()
-    finish(1, inputs, refs[18:27], results, forces, lambda: fields(results, 1), forced)
+    send(low_forces.reshape(3, CX, 8, NZ), targets[3], 0, 8)
+    finish(1, refs[:8], scratch, results, forces, lambda: fields(results, CY - 8))
+    send(forces.reshape(3, CX, 8, NZ), targets[3], CY - 8, 8)
     for copy in copies:
         copy.wait()
 
@@ -719,33 +704,28 @@
     own = [tv, ta, eu, *sizes, CX * 16, 19 * 8]
     own = [pltpu.VMEM((n, 128), F32) for n in own] + [pltpu.SMEM((24,), jnp.int32)]
     cost = pl.CostEstimate(flops=4_000_000, bytes_accessed=4_000_000, transcendentals=0)
-    *low, lm_next, mm_next, visc, body = pl.pallas_call(
+    low = pl.pallas_call(
         edge_low,
-        out_shape=[rows(3 * 64)] * 2 + [pltpu.HBM(s, F32) for s in shapes],
-        in_specs=[VMEM] * 10,
-        out_specs=[VMEM] * 2 + [HBM] * 4,
-        scratch_shapes=own + [pltpu.SemaphoreType.DMA((4,))],
+        out_shape=[rows(3 * 64)] * 2,
+        in_specs=[VMEM] * 8,
+        out_specs=[VMEM] * 2,
+        scratch_shapes=own,
         compiler_params=limit(16),
         cost_estimate=cost,
         name="edge_low",
-    )(up, first[2], ylow, *first[3:8], *first[:2])
-    given = [
-        pltpu.with_memory_space_constraint(value, pltpu.HBM)
-        for value in (lm_next, mm_next, visc, body)
-    ]
+    )(up, first[2], ylow, *first[3:8])
     return pl.pallas_call(
         edge_high,
         out_shape=[pltpu.HBM(s, F32) for s in shapes],
-        in_specs=[VMEM] * 10 + [HBM] * 4,
+        in_specs=[VMEM] * 12,
         out_specs=[HBM] * 4,
-        input_output_aliases={10 + i: i for i in range(4)},
         scratch_shapes=own
         + [pltpu.VMEM((3 * 64, 128), F32)] * 2
-        + [pltpu.SemaphoreType.DMA((8,))],
+        + [pltpu.SemaphoreType.DMA((12,))],
         compiler_params=limit(16),
         cost_estimate=cost,
         name="edge_high",
-    )(up, first[2], yhigh, *first[8:13], *low, *given)
+    )(up, first[2], yhigh, *first[8:13], *low, *first[:2])
 
 
 def solution(mesh):

time: 25.3 us -> 24.5 us (0.968)
  the two profiles are of different devices: /device:TPU:24 before, /device:TPU:8 now
where the time goes in v1:
time: 24.5 us; the launch traced here: 24.3 us
  starting transfers between devices  11.1 us (45%)
  Pallas kernels  7.12 us (29%)
  waiting for transfers between devices  4.78 us (20%)
  between operations  1.32 us (5%)
    ppermute x4, starting transfers between devices, shifted(): lax.ppermute(block, axis, [(i, (i + distance) % count) for i in range(cou...  11.1 us
    ppermute x4, waiting for transfers between devices, shifted(): lax.ppermute(block, axis, [(i, (i + distance) % count) for i in range(cou...  4.78 us
    pallas_call x1, Pallas kernels, shards(): pl.pallas_call(interior, out_shape=[rows(n) for n in (3 * field, 3 * fiel...  3.36 us
    pallas_call x1, Pallas kernels, shards(): pl.pallas_call(pack_x, out_shape=[rows(n) for n in (XMSG, XMSG, field, 16...  1.29 us
    pallas_call x1, Pallas kernels, shards(): pl.pallas_call(edge_high, out_shape=[pltpu.HBM(s, F32) for s in shapes],...  1.27 us
    pallas_call x1, Pallas kernels, shards(): pl.pallas_call(edge_low, out_shape=[rows(3 * 64)] * 2, in_specs=[VMEM] *...  1.04 us
  transfers between devices with their start and end apart: 4, of which 2 were waited for; matrix products, arithmetic and copies ran while one was open for 0% of the time, Pallas kernels for 18%

profile of v1, /device:TPU:8, one launch (start us, length us, event | category | flops | bytes accessed | tf_op | source)
XLA Modules:
  0.0 24.3 jit_solution(10531277244373629503)
XLA Ops:
  1.3 1.3 %pack_x.1 = (f32[496,128]{1,0:T(8,128)S(1)}, f32[496,128]{1,0:T(8,128)S(1)}, f32[256,128]{1,0:T(8,128)S(1)}, f32[16,128]{1,0:T(8,128)S(1)}, f32[768,128]{1,0:T(8...) custom-call(f32[768,128]{1,0:T(8,128)} %bitcast.9, f32[256,128]{1,0:T(8,128)} %bitcast.10, ...), custom_call_target="tpu_custom_call" | custom-call | tf_op jit(solution)/shard_map/pack_x/pallas_call | solution.py:662
  2.6 0.1 collective-permute-start
  2.7 5.3 %collective-permute-start.1 = (f32[496,128]{1,0:T(8,128)S(1)}, f32[496,128]{1,0:T(8,128)S(1)}, u32[]{:S(2)}, u32[]{:S(2)}) collective-permute-start(f32[496,128]{1,0:T(8,128)S(1)} %get-tuple-element.36), channel_id=1, source_target_pairs={{0,248},{8,0},{16,8},{24,16},{32,24},{40,32},{48,40},{56,48},{64,5... | collective-permute-start | bytes 761864 | tf_op jit(solution)/shard_map/ppermute | solution.py:23
  7.9 3.9 %collective-permute-done.xlow = f32[496,128]{1,0:T(8,128)S(1)} collective-permute-done((f32[496,128]{1,0:T(8,128)S(1)}, f32[496,128]{1,0:T(8,128)S(1)}, u32[]{:S(2)}, u32[]{:S(2)}) %collective-permute-start) | collective-permute-done | bytes 253984 | tf_op jit(solution)/shard_map/ppermute | solution.py:23
  11.8 0.0 collective-permute-done.1.xhigh
  11.8 0.0 copy-start
  11.8 0.2 pack_y.1
  12.0 2.7 %collective-permute-start.3 = (f32[272,128]{1,0:T(8,128)S(1)}, f32[272,128]{1,0:T(8,128)S(1)}, u32[]{:S(2)}, u32[]{:S(2)}) collective-permute-start(f32[272,128]{1,0:T(8,128)S(1)} %get-tuple-element.46), channel_id=1, source_target_pairs={{0,1},{1,2},{2,3},{3,4},{4,5},{5,6},{6,7},{7,0},{8,9},{9,10},{10,1... | collective-permute-start | bytes 417800 | tf_op jit(solution)/shard_map/ppermute | solution.py:23
  14.6 3.1 %collective-permute-start.2 = (f32[272,128]{1,0:T(8,128)S(1)}, f32[272,128]{1,0:T(8,128)S(1)}, u32[]{:S(2)}, u32[]{:S(2)}) collective-permute-start(f32[272,128]{1,0:T(8,128)S(1)} %get-tuple-element.40), channel_id=1, source_target_pairs={{0,7},{1,0},{2,1},{3,2},{4,3},{5,4},{6,5},{7,6},{8,15},{9,8},{10,9... | collective-permute-start | bytes 417800 | tf_op jit(solution)/shard_map/ppermute | solution.py:23
  17.7 0.0 copy-done
  17.7 3.4 %interior.1 = (f32[768,128]{1,0:T(8,128)S(1)}, f32[768,128]{1,0:T(8,128)S(1)}, f32[72,128]{1,0:T(8,128)S(1)}, f32[192,128]{1,0:T(8,128)S(1)}, f32[128,128]{1,0:T...) custom-call(f32[768,128]{1,0:T(8,128)S(1)} %get-tuple-element.30.vel, ...), custom_call_target="tpu_custom_call" | custom-call | flops 20000000 | bytes 20000000 | tf_op jit(solution)/shard_map/interior/pallas_call | solution.py:691
  21.1 0.0 collective-permute-done.3.refs_2_
  21.1 1.0 %edge_low.1 = (f32[192,128]{1,0:T(8,128)S(1)}, f32[192,128]{1,0:T(8,128)S(1)}) custom-call(s32[512,128]{1,0:T(8,128)S(1)} %bitcast.7, f32[72,128]{1,0:T(8,128)S(1)} %get-tuple-element.39.refs_1_, f32[272,128]{1,0:T(8,128)S(1)} %collective-permute-done.3.refs_2_, f32[192,128]{1,0:T(8,128)S(1)} %get-tuple-element.47.refs_3_, ...), custom_call_target="tpu_custom_call" | custom-call | flops 4000000 | bytes 4000000 | tf_op jit(solution)/shard_map/edge_low/pallas_call | solution.py:707
  22.1 0.9 %collective-permute-done.2.refs_2_ = f32[272,128]{1,0:T(8,128)S(1)} collective-permute-done((f32[272,128]{1,0:T(8,128)S(1)}, f32[272,128]{1,0:T(8,128)S(1)}, u32[]{:S(2)}, u32[]{:S(2)}) %collective-permute-start.2) | collective-permute-done | bytes 139296 | tf_op jit(solution)/shard_map/ppermute | solution.py:23
  23.0 1.3 %edge_high.1 = (f32[8,32,128]{2,1,0:T(8,128)}, f32[8,32,128]{2,1,0:T(8,128)}, f32[8,32,128]{2,1,0:T(8,128)}, f32[3,8,32,128]{3,2,1,0:T(8,128)}) custom-call(s32[512,128]{1,0:T(8,128)S(1)} %bitcast.8, f32[72,128]{1,0:T(8,128)S(1)} %get-tuple-element.39.refs_1_, f32[272,128]{1,0:T(8,128)S(1)} %collective-permute-done.2.refs_2_, ...), custom_call_target="tpu_custom_call" | custom-call | flops 4000000 | bytes 4000000 | tf_op jit(solution)/shard_map/edge_high/pallas_call | solution.py:717
Async XLA Ops:
  2.6 9.2 %collective-permute-start = (f32[496,128]{1,0:T(8,128)S(1)}, f32[496,128]{1,0:T(8,128)S(1)}, u32[]{:S(2)}, u32[]{:S(2)}) collective-permute-start(f32[496,128]{1,0:T(8,128)S(1)} %get-tuple-element.35), channel_id=1, source_target_pairs={{0,8},{8,16},{16,24},{24,32},{32,40},{40,48},{48,56},{56,64},{64,7... | collective-permute-start | bytes 761864 | tf_op jit(solution)/shard_map/ppermute | solution.py:23
  2.7 9.1 %collective-permute-start.1 = (f32[496,128]{1,0:T(8,128)S(1)}, f32[496,128]{1,0:T(8,128)S(1)}, u32[]{:S(2)}, u32[]{:S(2)}) collective-permute-start(f32[496,128]{1,0:T(8,128)S(1)} %get-tuple-element.36), channel_id=1, source_target_pairs={{0,248},{8,0},{16,8},{24,16},{32,24},{40,32},{48,40},{56,48},{64,5... | collective-permute-start | bytes 761864 | tf_op jit(solution)/shard_map/ppermute | solution.py:23
  11.8 5.9 %copy-start = (s32[2,8,32,128]{3,2,1,0:T(8,128)S(1)}, s32[2,8,32,128]{3,2,1,0:T(8,128)}, u32[]{:S(2)}) copy-start(s32[2,8,32,128]{3,2,1,0:T(8,128)} %param.10) | copy-start | bytes 786436
  12.0 9.1 %collective-permute-start.3 = (f32[272,128]{1,0:T(8,128)S(1)}, f32[272,128]{1,0:T(8,128)S(1)}, u32[]{:S(2)}, u32[]{:S(2)}) collective-permute-start(f32[272,128]{1,0:T(8,128)S(1)} %get-tuple-element.46), channel_id=1, source_target_pairs={{0,1},{1,2},{2,3},{3,4},{4,5},{5,6},{6,7},{7,0},{8,9},{9,10},{10,1... | collective-permute-start | bytes 417800 | tf_op jit(solution)/shard_map/ppermute | solution.py:23
  14.6 8.4 %collective-permute-start.2 = (f32[272,128]{1,0:T(8,128)S(1)}, f32[272,128]{1,0:T(8,128)S(1)}, u32[]{:S(2)}, u32[]{:S(2)}) collective-permute-start(f32[272,128]{1,0:T(8,128)S(1)} %get-tuple-element.40), channel_id=1, source_target_pairs={{0,7},{1,0},{2,1},{3,2},{4,3},{5,4},{6,5},{7,6},{8,15},{9,8},{10,9... | collective-permute-start | bytes 417800 | tf_op jit(solution)/shard_map/ppermute | solution.py:23
